TPU v7x, 32 devices: a whole 2x2x4 slice. The times are simulated.
32 devices in a mesh: parts: 2 (over x), elec: 4 (over y, core), walk: 4 (over z).
Axes of the slice: x: 2, y: 2, z: 4, core: 2. Of those that a mesh axis runs over, the one named last changes fastest.
Arguments:
- elec_pos: float32 [3, 32, 512], P(None, ('parts', 'walk'), 'elec'), parts along dimension 1, may hold values from -8 to 8
- atom_pos: float32 [200, 3], P(('parts', 'elec')), parts along dimension 0, may hold values from -8 to 8
- atom_emb: float32 [200, 256], P(('parts', 'elec')), parts along dimension 0, may hold values from -6 to 6
- spin_emb: float32 [2, 256], replicated, may hold values from -6 to 6
- spin: int32 [1024], P(('parts', 'elec')), parts along dimension 0, may hold values from 0 to 1, as said below
- near_atoms: int32 [16, 2], P('parts'), parts along dimension 0, may hold values from 0 to 3
- pair_list: int32 [16, 4], P('parts'), parts along dimension 0, may hold values from 0 to 7, as said below
- pair_count: int32 [16], P('parts'), parts along dimension 0, may hold values from 1 to 4, as said below
- w_query: bfloat16 [256, 256], replicated, may hold values from -64 to 64
- w_key: bfloat16 [256, 256], replicated, may hold values from -0.375 to 0.375
- w_value: bfloat16 [256, 256], replicated, may hold values from -0.375 to 0.375
- w_out: bfloat16 [256, 256], replicated, may hold values from -0.375 to 0.375
- w_orb: bfloat16 [2, 256, 1024], replicated, may hold values from -0.375 to 0.375
- target: bfloat16 [32, 512, 1024], P(('parts', 'walk'), 'elec'), parts along dimension 0, may hold values from -6 to 6
Outputs:
- grad_orb: float32 [4, 256, 1024], P('parts'), parts along dimension 0
- grad_out: float32 [512, 256], P('parts'), parts along dimension 0
- loss: float32 [2], P('parts'), parts along dimension 0
There are 2 independent parts, one for each index of `parts`. A program takes and returns all parts, laid end to end along the dimension named above; an argument that names none is the same for every part. Nothing has to cross between parts.
Inputs may be any that keep to these rules, and one draw needn't show every extreme that they name: `pair_list`: row b lists 4 distinct blocks, the first being b itself; every listed c has c // 2 equal to b // 2 or one more or one less than it, modulo 8 / 2. Only the first pair_count[b] entries of row b are listed; some block lists all 4. Each aligned run of 128 electrons holds exactly half of each spin.
All inputs are finite; a program needn't handle non-finite values.
Results may differ from a plain program's by a relative error of at most 0.002.
Values may be sent and summed in bfloat16 or wider, within the bound.
A program may use at most 64 MiB of HBM per device.

v0:
```python
import math
import jax
import jax.numpy as jnp
from jax import lax
from jax.sharding import PartitionSpec as P

HEADS = 16
BLOCK = 64
ATOM_DEV = 25
NEAR = 2
KMAX = 4


def shifted(block, axis, distance):
    devices = range(lax.axis_size(axis))
    route = [((i - distance) % len(devices), i) for i in devices]
    return lax.ppermute(block, axis, route)


def local(
    elec_pos,
    atom_pos,
    atom_emb,
    spin_emb,
    spin,
    near_atoms,
    pair_list,
    pair_count,
    w_query,
    w_key,
    w_value,
    w_out,
    w_orb,
    target,
):
    walkers = elec_pos.shape[1]
    local_rows = elec_pos.shape[2]
    per_device = local_rows // BLOCK
    elec_count = lax.axis_size("elec")
    elec_index = lax.axis_index("elec")
    model_width = w_query.shape[0]
    head_size = model_width // HEADS
    orbital_count = w_orb.shape[2]
    row_local = walkers * local_rows
    half_rows = local_rows // 2
    all_pos, all_emb = (
        lax.all_gather(atom_pos, "elec", axis=0, tiled=True),
        lax.all_gather(atom_emb, "elec", axis=0, tiled=True),
    )
    my_blocks = elec_index * per_device + jnp.arange(per_device)
    near_here = jnp.take(near_atoms, my_blocks, axis=0)
    near_pos = jnp.take(all_pos.reshape(elec_count, ATOM_DEV, 3), near_here, axis=0).reshape(
        per_device, NEAR * ATOM_DEV, 3
    )
    near_emb = jnp.take(
        all_emb.reshape(elec_count, ATOM_DEV, model_width), near_here, axis=0
    ).reshape(per_device, NEAR * ATOM_DEV, model_width)
    positions = elec_pos.reshape(3, walkers, per_device, BLOCK)
    distance = jnp.zeros((walkers, per_device, BLOCK, NEAR * ATOM_DEV), jnp.float32)
    for axis_id in range(3):
        spacing = positions[axis_id][..., None] - near_pos[None, :, None, :, axis_id]
        distance = distance + spacing * spacing
    closeness = 1.0 / (1.0 + distance)
    atom_term = jnp.einsum(
        "wbea,bad->wbed", closeness, near_emb, precision=lax.Precision.HIGHEST
    ).reshape(walkers, local_rows, model_width)
    spin_rows = jnp.where(spin[:, None] == 1, spin_emb[1][None, :], spin_emb[0][None, :])
    hidden = (atom_term + spin_rows[None]).astype(jnp.bfloat16)
    flat_rows = hidden.reshape(row_local, model_width)
    queries = (
        jnp.dot(flat_rows, w_query, preferred_element_type=jnp.float32)
        .astype(jnp.bfloat16)
        .reshape(walkers, local_rows, HEADS, head_size)
    )
    key_rows = (
        jnp.dot(flat_rows, w_key, preferred_element_type=jnp.float32)
        .astype(jnp.bfloat16)
        .reshape(walkers, local_rows, model_width)
    )
    value_rows = (
        jnp.dot(flat_rows, w_value, preferred_element_type=jnp.float32)
        .astype(jnp.bfloat16)
        .reshape(walkers, local_rows, model_width)
    )
    block_count = elec_count * per_device
    lists_here = jnp.take(pair_list, my_blocks, axis=0)
    counts_here = jnp.take(pair_count, my_blocks, axis=0)
    slot_ids = jnp.arange(KMAX)
    in_list = slot_ids[None, :] < counts_here[:, None]
    listed = jnp.any(
        (lists_here[:, :, None] == jnp.arange(block_count)[None, None, :]) & in_list[:, :, None],
        axis=1,
    )
    score_scale = 1.0 / math.sqrt(head_size)

    def attend_piece(running, key_part, value_part, key_blocks):
        old_max, old_total, old_acc = running
        key_count = key_part.shape[1]
        allowed = jnp.repeat(jnp.take(listed, key_blocks, axis=1), BLOCK, axis=0)
        key_mask = allowed[None, :, None, :]
        key_heads = key_part.reshape(walkers, key_count, HEADS, head_size)
        value_heads = value_part.reshape(walkers, key_count, HEADS, head_size)
        scores = (
            jnp.einsum("wqhd,wkhd->wqhk", queries, key_heads, preferred_element_type=jnp.float32)
            * score_scale
        )
        scores = jnp.where(key_mask, scores, -1e30)
        new_max = jnp.maximum(old_max, jnp.max(scores, axis=3))
        weights = jnp.where(key_mask, jnp.exp(scores - new_max[..., None]), 0.0)
        factor = jnp.exp(old_max - new_max)
        new_total = old_total * factor + jnp.sum(weights, axis=3)
        new_acc = old_acc * factor[..., None] + jnp.einsum(
            "wqhk,wkhd->wqhd",
            weights.astype(jnp.bfloat16),
            value_heads,
            preferred_element_type=jnp.float32,
        )
        return (new_max, new_total, new_acc)

    def shard_blocks(owner):
        return (owner * local_rows + jnp.arange(local_rows)) // BLOCK

    lower_owner = (elec_index + elec_count - 1) % elec_count
    upper_owner = (elec_index + 1) % elec_count
    initial = (
        jnp.full((walkers, local_rows, HEADS), -1e30, jnp.float32),
        jnp.zeros((walkers, local_rows, HEADS), jnp.float32),
        jnp.zeros((walkers, local_rows, HEADS, head_size), jnp.float32),
    )
    lower_kv = shifted((key_rows, value_rows), "elec", 1)
    upper_kv = shifted((key_rows, value_rows), "elec", -1)
    running = attend_piece(initial, key_rows, value_rows, shard_blocks(elec_index))
    running = attend_piece(running, lower_kv[0], lower_kv[1], shard_blocks(lower_owner))
    running = attend_piece(running, upper_kv[0], upper_kv[1], shard_blocks(upper_owner))
    final_max, final_total, final_acc = running
    attended = (
        (final_acc / final_total[..., None]).astype(jnp.bfloat16).reshape(row_local, model_width)
    )
    mixed_out = jnp.dot(attended, w_out, preferred_element_type=jnp.float32)
    hidden_out = (flat_rows.astype(jnp.float32) + mixed_out).astype(jnp.bfloat16)
    by_spin = jnp.argsort(spin, stable=True)
    sorted_hidden = jnp.take(hidden_out.reshape(walkers, local_rows, model_width), by_spin, axis=1)
    sorted_attended = jnp.take(attended.reshape(walkers, local_rows, model_width), by_spin, axis=1)
    sorted_target = jnp.take(target, by_spin, axis=1)
    loss_part = jnp.float32(0.0)
    orb_terms = []
    out_part = jnp.zeros((model_width, model_width), jnp.float32)
    for spin_id in range(2):
        hidden_group = sorted_hidden[:, spin_id * half_rows : (spin_id + 1) * half_rows].reshape(
            walkers * half_rows, model_width
        )
        attended_group = sorted_attended[
            :, spin_id * half_rows : (spin_id + 1) * half_rows
        ].reshape(walkers * half_rows, model_width)
        target_group = sorted_target[:, spin_id * half_rows : (spin_id + 1) * half_rows].reshape(
            walkers * half_rows, orbital_count
        )
        orbitals = jnp.dot(hidden_group, w_orb[spin_id], preferred_element_type=jnp.float32)
        residual = orbitals - target_group.astype(jnp.float32)
        loss_part = loss_part + 0.5 * jnp.sum(residual * residual)
        signal = residual.astype(jnp.bfloat16)
        orb_terms.append(
            lax.dot_general(
                hidden_group, signal, (((0,), (0,)), ((), ())), preferred_element_type=jnp.float32
            )
        )
        backward = lax.dot_general(
            signal, w_orb[spin_id], (((1,), (1,)), ((), ())), preferred_element_type=jnp.float32
        ).astype(jnp.bfloat16)
        out_part = out_part + lax.dot_general(
            attended_group, backward, (((0,), (0,)), ((), ())), preferred_element_type=jnp.float32
        )
    orb_part = jnp.stack(orb_terms, axis=0)
    orb_sum, out_sum, loss_sum = lax.psum((orb_part, out_part, loss_part), ("elec", "walk"))
    rows_float = jnp.float32(row_local * elec_count * lax.axis_size("walk"))
    grad_orb = orb_sum / rows_float
    grad_out = out_sum / rows_float
    loss = jnp.reshape(loss_sum / rows_float, (1,))
    return (grad_orb, grad_out, loss)


def solution(mesh):
    in_specs = (
        P(None, ("parts", "walk"), "elec"),
        P(("parts", "elec"), None),
        P(("parts", "elec"), None),
        P(),
        P(("parts", "elec")),
        P("parts", None),
        P("parts", None),
        P("parts"),
        P(),
        P(),
        P(),
        P(),
        P(),
        P(("parts", "walk"), "elec", None),
    )
    out_specs = (P("parts", None, None), P("parts", None), P("parts"))
    return jax.shard_map(local, mesh=mesh, in_specs=in_specs, out_specs=out_specs, check_vma=False)
```

profile of v0, /device:TPU:0, one launch (start us, length us, event | category | flops | bytes accessed | tf_op | source)
XLA Modules:
  0.0 197.2 jit_solution(5505594694340146671)
XLA Ops:
  9.0 6.3 %all-gather.1 = f32[4,25,3]{1,2,0:T(4,128)S(1)} all-gather(f32[1,25,3]{1,2,0:T(4,128)} %bitcast.217), channel_id=1, replica_groups=mesh['parts'=2,'elec'=4,'walk'=4] {'elec'}, dimensions={0}, use_global_device_ids=true | all-gather | bytes 1500 | tf_op jit(solution)/shard_map/all_gather | solution.py:47
  16.1 5.8 %all-gather = f32[4,25,256]{2,1,0:T(8,128)S(1)} all-gather(f32[1,25,256]{2,1,0:T(8,128)} %bitcast.214), channel_id=1, replica_groups=mesh['parts'=2,'elec'=4,'walk'=4] {'elec'}, dimensions={0}, use_global_device_ids=true | all-gather | bytes 128000 | tf_op jit(solution)/shard_map/all_gather | solution.py:48
  26.6 1.4 collective-permute-start.2
  29.3 2.5 %sort.17 = (s32[128]{0:T(128)}, s32[128]{0:T(128)S(1)}) sort(s32[128]{0:T(128)S(1)} %copy-done.14, s32[128]{0:T(128)S(1)} %iota.37), dimensions={0}, to_apply=%region_7.9 | sort | flops 896 | bytes 2048 | tf_op jit(solution)/shard_map/jit(argsort)/sort | solution.py:141
  37.9 3.7 %gather_fusion.5 = bf16[128,4,1024]{2,0,1:T(8,128)(2,1)S(1)} fusion(bf16[4,128,1024]{2,1,0:T(8,128)(2,1)S(1)} %copy-done, s32[1024]{0:T(1024)S(1)} %pad_clamp_fusion), kind=kCustom, calls=%fused_computation.10 | custom fusion | bytes 2097664 | tf_op jit(solution)/shard_map/jit(_take)/gather | solution.py:144
  41.7 2.9 %fusion = (f32[4,128,16]{1,2,0:T(8,128)S(1)}, f32[4,16,128,128]{3,2,1,0:T(8,128)}) fusion(pred[128,128]{0,1:T(8,128)(4,1)S(1)} %copy.146, bf16[4,128,16,16]{1,0,3,2:T(4,128)(2,1)S(1)} %reshape.316, bf16[4,128,16,16]{1,0,3,2:T(4,128)(2,1)S(1)} %reshape_reshape.9), kind=kOutput, calls=%fused_computation.17 | convolution fusion | flops 36691968 | bytes 4767744 | tf_op jit(solution)/shard_map/wqhd,wkhd->wqhk/dot_general | solution.py:104
  44.6 1.1 fusion.117
  45.7 1.1 copy.157
  46.9 2.8 %fusion.1 = (f32[4,128,16]{1,2,0:T(8,128)S(1)}, f32[4,16,128,128]{3,2,1,0:T(8,128)}) fusion(pred[128,128]{0,1:T(8,128)(4,1)S(1)} %copy.156, bf16[4,128,16,16]{1,3,2,0:T(8,128)(2,1)S(1)} %bitcast.193, bf16[4,128,16,16]{1,0,3,2:T(4,128)(2,1)S(1)} %reshape.316), kind=kOutput, calls=%fused_computation.18 | convolution fusion | flops 36691968 | bytes 4767744 | tf_op jit(solution)/shard_map/wqhd,wkhd->wqhk/dot_general | solution.py:104
  51.8 1.3 fusion.7
  53.7 2.1 %copy-done.3 = f32[4,16,128,128]{3,2,1,0:T(8,128)S(1)} copy-done((f32[4,16,128,128]{3,2,1,0:T(8,128)S(1)}, f32[4,16,128,128]{3,2,1,0:T(8,128)}, u32[]{:S(2)}) %copy-start.3) | copy-done | bytes 4194328
  55.8 2.3 %fusion.3 = (f32[4,128,16]{1,2,0:T(8,128)S(1)}, f32[4,128,16]{1,2,0:T(8,128)S(1)}) fusion(f32[4,16,128,128]{3,2,1,0:T(8,128)S(1)} %copy-done.3, f32[4,128,16]{1,2,0:T(8,128)S(1)} %get-tuple-element.21, pred[128,128]{0,1:T(8,128)(4,1)S(1)} %copy.146, f32[4,128,16]{1,2,0:T(8,128)S(1)} %get-tuple-element.13, f32[4,16,128,128]{3,2,1,0:T(8,128)S(1)} %copy-done.2, ...), kind=kLoop, calls=%fused_computation.20 | loop fusion | flops 10469376 | bytes 8552448 | tf_op jit(solution)/shard_map/reduce_sum | solution.py:111
  58.2 1.8 fusion.33
  61.1 3.1 %fusion.24 = f32[4,128,16,16]{1,3,2,0:T(8,128)S(1)} fusion(bf16[4,128,16,16]{1,3,2,0:T(8,128)(2,1)S(1)} %bitcast.207, f32[4,16,128,128]{3,2,1,0:T(8,128)} %copy-done.4, f32[4,128,16]{1,2,0:T(8,128)S(1)} %get-tuple-element.12, pred[128,128]{0,1:T(8,128)(4,1)S(1)} %copy.163), kind=kOutput, calls=%fused_computation.39 | convolution fusion | flops 38797312 | bytes 5029888 | tf_op jit(solution)/shard_map/wqhk,wkhd->wqhd/dot_general | solution.py:112
  64.2 1.1 copy.159
  65.3 3.3 %fusion.47 = bf16[4,128,16,16]{1,3,2,0:T(8,128)(2,1)S(1)} fusion(f32[4,128,16,16]{1,3,2,0:T(8,128)S(1)} %fusion.24, f32[4,128,16,16]{1,3,2,0:T(8,128)} %fusion.33, bf16[4,128,16,16]{1,3,2,0:T(8,128)(2,1)S(1)} %bitcast.206, f32[4,16,128,128]{3,2,1,0:T(8,128)} %get-tuple-element.35, f32[4,128,16]{1,2,0:T(8,128)S(1)} %get-tuple-element.13, ...), kind=kOutput, calls=%fused_computation.60 | convolution fusion | flops 39452672 | bytes 5881856 | tf_op jit(solution)/shard_map/wqhk,wkhd->wqhd/dot_general | solution.py:112
  71.9 2.2 %multiply_reduce_fusion.1 = (f32[]{:T(128)}, bf16[256,1024]{1,0:T(8,128)(2,1)S(1)}) fusion(bf16[256,1024]{1,0:T(8,128)(2,1)} %bitcast.200, bf16[256,256]{1,0:T(8,128)(2,1)S(1)} %bitcast.203, bf16[2,256,1024]{2,1,0:T(8,128)(2,1)} %param.30), kind=kOutput, calls=%fused_computation.57 | convolution fusion | flops 135528448 | bytes 1703940 | tf_op jit(solution)/shard_map/dot_general | solution.py:158
  74.4 2.3 %fusion.43 = f32[256,256]{1,0:T(8,128)} fusion(bf16[256,256]{1,0:T(8,128)(2,1)S(1)} %bitcast.210, bf16[2,256,1024]{2,1,0:T(8,128)(2,1)} %param.30, bf16[256,1024]{1,0:T(8,128)(2,1)S(1)} %get-tuple-element.39), kind=kOutput, calls=%fused_computation.54 | convolution fusion | flops 167837696 | bytes 1441792 | tf_op jit(solution)/shard_map/dot_general | solution.py:170
  76.8 2.1 %multiply_reduce_fusion = (f32[]{:T(128)}, bf16[256,1024]{1,0:T(8,128)(2,1)S(1)}) fusion(bf16[256,1024]{1,0:T(8,128)(2,1)S(1)} %bitcast.199, bf16[256,256]{1,0:T(8,128)(2,1)S(1)} %bitcast.201, bf16[2,256,1024]{2,1,0:T(8,128)(2,1)} %param.30), kind=kOutput, calls=%fused_computation.56 | convolution fusion | flops 135528448 | bytes 1703940 | tf_op jit(solution)/shard_map/dot_general | solution.py:158
  80.0 2.5 %convolution_add_fusion.1 = f32[256,256]{1,0:T(8,128)} fusion(f32[256,256]{1,0:T(8,128)} %fusion.43, bf16[256,256]{1,0:T(8,128)(2,1)S(1)} %bitcast.205, bf16[2,256,1024]{2,1,0:T(8,128)(2,1)} %param.30, bf16[256,1024]{1,0:T(8,128)(2,1)} %copy-done.5), kind=kOutput, calls=%fused_computation.51 | convolution fusion | flops 167903232 | bytes 1703936 | tf_op jit(solution)/shard_map/dot_general | solution.py:170
  82.5 1.5 pad_maximum_fusion
  85.2 35.5 %psum.23 = f32[]{:T(128)} all-reduce(f32[]{:T(128)S(6)} %add.215), channel_id=1, replica_groups=mesh['parts'=2,'elec'=4,'walk'=4] {'elec','walk'}, use_global_device_ids=true, to_apply=%region_12.15 | all-reduce | flops 1 | bytes 8 | tf_op jit(solution)/shard_map/psum | solution.py:174
  121.4 63.9 %all-reduce.3.cloned.1.call-done = (f32[2,256,1024]{2,1,0:T(8,128)}, f32[256,256]{1,0:T(8,128)}) async-done(((f32[2,256,1024]{2,1,0:T(8,128)}, f32[256,256]{1,0:T(8,128)}), (f32[2,256,1024]{2,1,0:T(8,128)}, f32[256,256]{1,0:T(8,128)})) %all-reduce.3.cloned.1.call-update) | async-done | bytes 2359312 | tf_op jit(solution)/shard_map/psum | solution.py:174
  185.2 3.3 %broadcast_multiply_fusion = f32[2,256,1024]{2,1,0:T(8,128)} fusion(f32[2,256,1024]{2,1,0:T(8,128)} %get-tuple-element.7), kind=kLoop, calls=%fused_computation.58 | loop fusion | flops 524288 | bytes 4194304 | tf_op jit(solution)/shard_map/div | solution.py:176
  (136 shorter events, 23.5 us)
Async XLA Ops:
  7.2 30.7 %copy-start = (bf16[4,128,1024]{2,1,0:T(8,128)(2,1)S(1)}, bf16[4,128,1024]{2,1,0:T(8,128)(2,1)}, u32[]{:S(2)}) copy-start(bf16[4,128,1024]{2,1,0:T(8,128)(2,1)} %param.31) | copy-start | bytes 3145732
  7.2 22.1 %copy-start.14 = (s32[128]{0:T(128)S(1)}, s32[128]{0:T(128)}, u32[]{:S(2)}) copy-start(s32[128]{0:T(128)} %param.22) | copy-start | bytes 1540
  7.2 18.8 %copy-start.9 = (bf16[256,256]{1,0:T(8,128)(2,1)S(1)}, bf16[256,256]{1,0:T(8,128)(2,1)}, u32[]{:S(2)}) copy-start(bf16[256,256]{1,0:T(8,128)(2,1)} %param.27) | copy-start | bytes 393220
  7.2 20.8 %copy-start.10 = (bf16[256,256]{1,0:T(8,128)(2,1)S(1)}, bf16[256,256]{1,0:T(8,128)(2,1)}, u32[]{:S(2)}) copy-start(bf16[256,256]{1,0:T(8,128)(2,1)} %param.28) | copy-start | bytes 393220
  7.2 24.6 %copy-start.12 = (s32[8,4]{0,1:T(4,128)S(1)}, s32[8,4]{0,1:T(4,128)}, u32[]{:S(2)}) copy-start(s32[8,4]{0,1:T(4,128)} %param.24) | copy-start | bytes 388
  7.2 25.3 %copy-start.1 = (s32[8]{0:T(128)S(1)}, s32[8]{0:T(128)}, u32[]{:S(2)}) copy-start(s32[8]{0:T(128)} %param.25) | copy-start | bytes 100
  7.2 27.3 %copy-start.11 = (bf16[256,256]{1,0:T(8,128)(2,1)S(1)}, bf16[256,256]{1,0:T(8,128)(2,1)}, u32[]{:S(2)}) copy-start(bf16[256,256]{1,0:T(8,128)(2,1)} %param.26) | copy-start | bytes 393220
  7.2 178.0 %all-reduce.3.cloned.1.call-start = ((), (), s32[]{:S(2)}) async-start(), calls=%async_computation | async-start | bytes 4718592 | tf_op jit(solution)/shard_map/psum | solution.py:174
  26.2 19.6 %collective-permute-start = (bf16[4,128,256]{2,1,0:T(8,128)(2,1)S(1)}, bf16[4,128,256]{2,1,0:T(8,128)(2,1)}, u32[]{:S(2)}, u32[]{:S(2)}) collective-permute-start(bf16[4,128,256]{2,1,0:T(8,128)(2,1)S(1)} %bitcast.196), channel_id=1, source_target_pairs={{12,0},{0,4},{4,8},{8,12},{13,1},{1,5},{5,9},{9,13},{14,2},{2,6},{... | collective-permute-start | bytes 786440 | tf_op jit(solution)/shard_map/ppermute | solution.py:17
  26.6 23.1 %collective-permute-start.2 = (bf16[4,128,256]{2,1,0:T(8,128)(2,1)S(1)}, bf16[4,128,256]{2,1,0:T(8,128)(2,1)}, u32[]{:S(2)}, u32[]{:S(2)}) collective-permute-start(bf16[4,128,256]{2,1,0:T(8,128)(2,1)S(1)} %bitcast.197), channel_id=1, source_target_pairs={{4,0},{8,4},{12,8},{0,12},{5,1},{9,5},{13,9},{1,13},{6,2},{10,6},{... | collective-permute-start | bytes 786440 | tf_op jit(solution)/shard_map/ppermute | solution.py:17
  28.3 31.7 %collective-permute-start.3 = (bf16[4,128,256]{2,1,0:T(8,128)(2,1)S(1)}, bf16[4,128,256]{2,1,0:T(8,128)(2,1)}, u32[]{:S(2)}, u32[]{:S(2)}) collective-permute-start(bf16[4,128,256]{2,1,0:T(8,128)(2,1)S(1)} %bitcast.194), channel_id=1, source_target_pairs={{4,0},{8,4},{12,8},{0,12},{5,1},{9,5},{13,9},{1,13},{6,2},{10,6},{... | collective-permute-start | bytes 786440 | tf_op jit(solution)/shard_map/ppermute | solution.py:17
  28.7 35.4 %collective-permute-start.1 = (bf16[4,128,256]{2,1,0:T(8,128)(2,1)S(1)}, bf16[4,128,256]{2,1,0:T(8,128)(2,1)}, u32[]{:S(2)}, u32[]{:S(2)}) collective-permute-start(bf16[4,128,256]{2,1,0:T(8,128)(2,1)S(1)} %bitcast.195), channel_id=1, source_target_pairs={{12,0},{0,4},{4,8},{8,12},{13,1},{1,5},{5,9},{9,13},{14,2},{2,6},{... | collective-permute-start | bytes 786440 | tf_op jit(solution)/shard_map/ppermute | solution.py:17
  50.8 2.9 %copy-start.2 = (f32[4,16,128,128]{3,2,1,0:T(8,128)S(1)}, f32[4,16,128,128]{3,2,1,0:T(8,128)}, u32[]{:S(2)}) copy-start(f32[4,16,128,128]{3,2,1,0:T(8,128)} %get-tuple-element.35) | copy-start | bytes 12582916
  50.8 5.0 %copy-start.3 = (f32[4,16,128,128]{3,2,1,0:T(8,128)S(1)}, f32[4,16,128,128]{3,2,1,0:T(8,128)}, u32[]{:S(2)}) copy-start(f32[4,16,128,128]{3,2,1,0:T(8,128)} %get-tuple-element.37) | copy-start | bytes 12582916
  51.8 6.3 %copy-start.4 = (f32[4,16,128,128]{3,2,1,0:T(8,128)}, f32[4,16,128,128]{3,2,1,0:T(8,128)S(1)}, u32[]{:S(2)}) copy-start(f32[4,16,128,128]{3,2,1,0:T(8,128)S(1)} %get-tuple-element.33) | copy-start | bytes 12582916
  55.8 2.3 %copy-start.7 = (bf16[4,128,16,16]{1,0,3,2:T(4,128)(2,1)S(1)}, bf16[4,128,16,16]{1,0,3,2:T(4,128)(2,1)}, u32[]{:S(2)}) copy-start(bf16[4,128,16,16]{1,0,3,2:T(4,128)(2,1)} %reshape_reshape.10) | copy-start | bytes 786436
  65.3 3.6 %copy-start.13 = (bf16[256,256]{1,0:T(8,128)(2,1)S(1)}, bf16[256,256]{1,0:T(8,128)(2,1)}, u32[]{:S(2)}) copy-start(bf16[256,256]{1,0:T(8,128)(2,1)} %param.29) | copy-start | bytes 393220
  71.2 5.5 %copy-start.6 = (bf16[4,64,1024]{2,1,0:T(8,128)(2,1)S(1)}, bf16[4,64,1024]{2,1,0:T(8,128)(2,1)}, u32[]{:S(2)}) copy-start(bf16[4,64,1024]{2,1,0:T(8,128)(2,1)} %get-tuple-element.15) | copy-start | bytes 1572868
  78.8 0.8 copy-start.5
  185.2 3.3 %copy-start.8 = (f32[256,256]{1,0:T(8,128)S(1)}, f32[256,256]{1,0:T(8,128)}, u32[]{:S(2)}) copy-start(f32[256,256]{1,0:T(8,128)} %get-tuple-element.8) | copy-start | bytes 786436
Sparse Core Ops, SparseCore 0:
  84.1 101.0 all-reduce.2
where the time goes:
time: 198 us; the launch traced here: 197 us
  waiting for transfers between devices  63.9 us (32%)
  blocking collectives  47.7 us (24%)
  matrix products  26.4 us (13%)
  local copies, waits for them, and re-layouts  25.5 us (13%)
  between operations  17.6 us (9%)
  other arithmetic  13.7 us (7%)
  starting transfers between devices  2.44 us (1%)
    psum x1, waiting for transfers between devices, local(): lax.psum((orb_part, out_part, loss_part), ('elec', 'walk'))  63.9 us
    psum x1, blocking collectives, local(): lax.psum((orb_part, out_part, loss_part), ('elec', 'walk'))  35.5 us
    dot_general x3, matrix products, attend_piece(): jnp.einsum('wqhk,wkhd->wqhd', weights.astype(jnp.bfloat16), value_heads,...  8.22 us
    dot_general x3, matrix products, attend_piece(): jnp.einsum('wqhd,wkhd->wqhk', queries, key_heads, preferred_element_type=...  6.68 us
    all_gather x1, blocking collectives, local(): lax.all_gather(atom_pos, 'elec', axis=0, tiled=True)  6.28 us
    all_gather x1, blocking collectives, local(): lax.all_gather(atom_emb, 'elec', axis=0, tiled=True)  5.85 us
    dot_general x2, matrix products, local(): lax.dot_general(attended_group, backward, (((0,), (0,)), ((), ())), prefe...  4.87 us
    unnamed x32, local copies, waits for them, and re-layouts  4.51 us
  transfers between devices with their start and end apart: 5, of which 1 were waited for; matrix products, arithmetic and copies ran while one was open for 16% of the time, Pallas kernels for 0%

commit v1 on v0

--- a/solution.py
+++ b/solution.py
@@ -171,7 +171,7 @@
             attended_group, backward, (((0,), (0,)), ((), ())), preferred_element_type=jnp.float32
         )
     orb_part = jnp.stack(orb_terms, axis=0)
-    orb_sum, out_sum, loss_sum = lax.psum((orb_part, out_part, loss_part), ("elec", "walk"))
+    orb_sum, out_sum, loss_sum = lax.psum(lax.psum((orb_part, out_part, loss_part), "walk"), "elec")
     rows_float = jnp.float32(row_local * elec_count * lax.axis_size("walk"))
     grad_orb = orb_sum / rows_float
     grad_out = out_sum / rows_float

time: 198 us -> 252 us (1.27)
  waiting for transfers between devices: 63.9 us -> 136 us
  blocking collectives: 47.7 us -> 29.3 us
    psum x1 -> x2, waiting for transfers between devices: 63.9 us -> 136 us  [the longest x1 97.6 us: local(): lax.psum((orb_part, out_part, loss_part), 'walk')]
    psum x1 -> x2, blocking collectives: 35.5 us -> 17.1 us  [the longest x1 9.98 us: local(): lax.psum((orb_part, out_part, loss_part), 'walk')]
  transfers between devices with their start and end apart: 5 -> 6, of which waited for: 1 -> 2; matrix products, arithmetic and copies ran while one was open for 16% -> 13% of each run, Pallas kernels for 0% -> 0%
where the time goes in v1:
time: 252 us; the launch traced here: 251 us
  waiting for transfers between devices  136 us (54%)
  blocking collectives  29.3 us (12%)
  matrix products  26.4 us (10%)
  local copies, waits for them, and re-layouts  25.5 us (10%)
  between operations  17.6 us (7%)
  other arithmetic  13.7 us (5%)
    psum x1, waiting for transfers between devices, local(): lax.psum((orb_part, out_part, loss_part), 'walk')  97.6 us
    psum x1, waiting for transfers between devices, local(): lax.psum(lax.psum((orb_part, out_part, loss_part), 'walk'), 'elec')  38.5 us
    psum x1, blocking collectives, local(): lax.psum((orb_part, out_part, loss_part), 'walk')  9.98 us
    dot_general x3, matrix products, attend_piece(): jnp.einsum('wqhk,wkhd->wqhd', weights.astype(jnp.bfloat16), value_heads,...  8.22 us
    psum x1, blocking collectives, local(): lax.psum(lax.psum((orb_part, out_part, loss_part), 'walk'), 'elec')  7.16 us
    dot_general x3, matrix products, attend_piece(): jnp.einsum('wqhd,wkhd->wqhk', queries, key_heads, preferred_element_type=...  6.68 us
    all_gather x1, blocking collectives, local(): lax.all_gather(atom_pos, 'elec', axis=0, tiled=True)  6.28 us
    all_gather x1, blocking collectives, local(): lax.all_gather(atom_emb, 'elec', axis=0, tiled=True)  5.85 us
  transfers between devices with their start and end apart: 6, of which 2 were waited for; matrix products, arithmetic and copies ran while one was open for 13% of the time, Pallas kernels for 0%

profile of v1, /device:TPU:0, one launch (start us, length us, event | category | flops | bytes accessed | tf_op | source)
XLA Modules:
  0.0 251.1 jit_solution(1149727703964630522)
XLA Ops:
  9.0 6.3 %all-gather.1 = f32[4,25,3]{1,2,0:T(4,128)S(1)} all-gather(f32[1,25,3]{1,2,0:T(4,128)} %bitcast.217), channel_id=1, replica_groups=mesh['parts'=2,'elec'=4,'walk'=4] {'elec'}, dimensions={0}, use_global_device_ids=true | all-gather | bytes 1500 | tf_op jit(solution)/shard_map/all_gather | solution.py:47
  16.1 5.8 %all-gather = f32[4,25,256]{2,1,0:T(8,128)S(1)} all-gather(f32[1,25,256]{2,1,0:T(8,128)} %bitcast.214), channel_id=1, replica_groups=mesh['parts'=2,'elec'=4,'walk'=4] {'elec'}, dimensions={0}, use_global_device_ids=true | all-gather | bytes 128000 | tf_op jit(solution)/shard_map/all_gather | solution.py:48
  26.6 1.4 collective-permute-start.2
  29.3 2.5 %sort.17 = (s32[128]{0:T(128)}, s32[128]{0:T(128)S(1)}) sort(s32[128]{0:T(128)S(1)} %copy-done.14, s32[128]{0:T(128)S(1)} %iota.37), dimensions={0}, to_apply=%region_7.9 | sort | flops 896 | bytes 2048 | tf_op jit(solution)/shard_map/jit(argsort)/sort | solution.py:141
  37.9 3.7 %gather_fusion.5 = bf16[128,4,1024]{2,0,1:T(8,128)(2,1)S(1)} fusion(bf16[4,128,1024]{2,1,0:T(8,128)(2,1)S(1)} %copy-done, s32[1024]{0:T(1024)S(1)} %pad_clamp_fusion), kind=kCustom, calls=%fused_computation.10 | custom fusion | bytes 2097664 | tf_op jit(solution)/shard_map/jit(_take)/gather | solution.py:144
  41.7 2.9 %fusion = (f32[4,128,16]{1,2,0:T(8,128)S(1)}, f32[4,16,128,128]{3,2,1,0:T(8,128)}) fusion(pred[128,128]{0,1:T(8,128)(4,1)S(1)} %copy.146, bf16[4,128,16,16]{1,0,3,2:T(4,128)(2,1)S(1)} %reshape.316, bf16[4,128,16,16]{1,0,3,2:T(4,128)(2,1)S(1)} %reshape_reshape.9), kind=kOutput, calls=%fused_computation.17 | convolution fusion | flops 36691968 | bytes 4767744 | tf_op jit(solution)/shard_map/wqhd,wkhd->wqhk/dot_general | solution.py:104
  46.9 2.8 %fusion.1 = (f32[4,128,16]{1,2,0:T(8,128)S(1)}, f32[4,16,128,128]{3,2,1,0:T(8,128)}) fusion(pred[128,128]{0,1:T(8,128)(4,1)S(1)} %copy.156, bf16[4,128,16,16]{1,3,2,0:T(8,128)(2,1)S(1)} %bitcast.193, bf16[4,128,16,16]{1,0,3,2:T(4,128)(2,1)S(1)} %reshape.316), kind=kOutput, calls=%fused_computation.18 | convolution fusion | flops 36691968 | bytes 4767744 | tf_op jit(solution)/shard_map/wqhd,wkhd->wqhk/dot_general | solution.py:104
  51.8 1.3 fusion.7
  53.7 2.1 copy-done.3
  55.8 2.3 fusion.3
  58.2 1.8 fusion.33
  61.1 3.1 %fusion.24 = f32[4,128,16,16]{1,3,2,0:T(8,128)S(1)} fusion(bf16[4,128,16,16]{1,3,2,0:T(8,128)(2,1)S(1)} %bitcast.207, f32[4,16,128,128]{3,2,1,0:T(8,128)} %copy-done.4, f32[4,128,16]{1,2,0:T(8,128)S(1)} %get-tuple-element.14, pred[128,128]{0,1:T(8,128)(4,1)S(1)} %copy.163), kind=kOutput, calls=%fused_computation.39 | convolution fusion | flops 38797312 | bytes 5029888 | tf_op jit(solution)/shard_map/wqhk,wkhd->wqhd/dot_general | solution.py:112
  64.2 1.1 copy.159
  65.3 3.3 %fusion.47 = bf16[4,128,16,16]{1,3,2,0:T(8,128)(2,1)S(1)} fusion(f32[4,128,16,16]{1,3,2,0:T(8,128)S(1)} %fusion.24, f32[4,128,16,16]{1,3,2,0:T(8,128)} %fusion.33, bf16[4,128,16,16]{1,3,2,0:T(8,128)(2,1)S(1)} %bitcast.206, f32[4,16,128,128]{3,2,1,0:T(8,128)} %get-tuple-element.37, f32[4,128,16]{1,2,0:T(8,128)S(1)} %get-tuple-element.15, ...), kind=kOutput, calls=%fused_computation.60 | convolution fusion | flops 39452672 | bytes 5881856 | tf_op jit(solution)/shard_map/wqhk,wkhd->wqhd/dot_general | solution.py:112
  71.9 2.2 multiply_reduce_fusion.1
  74.4 2.3 fusion.43
  76.7 2.1 multiply_reduce_fusion
  79.9 2.5 %convolution_add_fusion.1 = f32[256,256]{1,0:T(8,128)} fusion(f32[256,256]{1,0:T(8,128)} %fusion.43, bf16[256,256]{1,0:T(8,128)(2,1)S(1)} %bitcast.205, bf16[2,256,1024]{2,1,0:T(8,128)(2,1)} %param.30, bf16[256,1024]{1,0:T(8,128)(2,1)} %copy-done.5), kind=kOutput, calls=%fused_computation.51 | convolution fusion | flops 167903232 | bytes 1703936 | tf_op jit(solution)/shard_map/dot_general | solution.py:170
  82.5 1.5 pad_maximum_fusion
  84.0 97.6 %all-reduce.5.cloned.1.call-done = (f32[2,256,1024]{2,1,0:T(8,128)}, f32[256,256]{1,0:T(8,128)}) async-done(((f32[2,256,1024]{2,1,0:T(8,128)}, f32[256,256]{1,0:T(8,128)}), (f32[2,256,1024]{2,1,0:T(8,128)}, f32[256,256]{1,0:T(8,128)})) %all-reduce.5.cloned.1.call-update) | async-done | bytes 2359312 | tf_op jit(solution)/shard_map/psum | solution.py:174
  182.8 10.0 %psum.46 = f32[]{:T(128)} all-reduce(f32[]{:T(128)S(6)} %add.221), channel_id=1, replica_groups=mesh['parts'=2,'elec'=4,'walk'=4] {'walk'}, use_global_device_ids=true, to_apply=%region_14.17 | all-reduce | flops 1 | bytes 8 | tf_op jit(solution)/shard_map/psum | solution.py:174
  192.8 7.2 %psum.47 = f32[]{:T(128)} all-reduce(f32[]{:T(128)} %psum.46), channel_id=1, replica_groups=mesh['parts'=2,'elec'=4,'walk'=4] {'elec'}, use_global_device_ids=true, to_apply=%region_15.18 | all-reduce | flops 1 | bytes 8 | tf_op jit(solution)/shard_map/psum | solution.py:174
  200.6 38.5 %all-reduce.7.cloned.1.call-done = (f32[2,256,1024]{2,1,0:T(8,128)}, f32[256,256]{1,0:T(8,128)}) async-done(((f32[2,256,1024]{2,1,0:T(8,128)}, f32[256,256]{1,0:T(8,128)}), (f32[2,256,1024]{2,1,0:T(8,128)}, f32[256,256]{1,0:T(8,128)})) %all-reduce.7.cloned.1.call-update) | async-done | bytes 2359312 | tf_op jit(solution)/shard_map/psum | solution.py:174
  239.1 3.3 %broadcast_multiply_fusion = f32[2,256,1024]{2,1,0:T(8,128)} fusion(f32[2,256,1024]{2,1,0:T(8,128)} %get-tuple-element.9), kind=kLoop, calls=%fused_computation.58 | loop fusion | flops 524288 | bytes 4194304 | tf_op jit(solution)/shard_map/div | solution.py:176
  (140 shorter events, 25.8 us)
Async XLA Ops:
  7.2 30.7 %copy-start = (bf16[4,128,1024]{2,1,0:T(8,128)(2,1)S(1)}, bf16[4,128,1024]{2,1,0:T(8,128)(2,1)}, u32[]{:S(2)}) copy-start(bf16[4,128,1024]{2,1,0:T(8,128)(2,1)} %param.31) | copy-start | bytes 3145732
  7.2 22.1 %copy-start.14 = (s32[128]{0:T(128)S(1)}, s32[128]{0:T(128)}, u32[]{:S(2)}) copy-start(s32[128]{0:T(128)} %param.22) | copy-start | bytes 1540
  7.2 18.8 %copy-start.9 = (bf16[256,256]{1,0:T(8,128)(2,1)S(1)}, bf16[256,256]{1,0:T(8,128)(2,1)}, u32[]{:S(2)}) copy-start(bf16[256,256]{1,0:T(8,128)(2,1)} %param.27) | copy-start | bytes 393220
  7.2 20.8 %copy-start.10 = (bf16[256,256]{1,0:T(8,128)(2,1)S(1)}, bf16[256,256]{1,0:T(8,128)(2,1)}, u32[]{:S(2)}) copy-start(bf16[256,256]{1,0:T(8,128)(2,1)} %param.28) | copy-start | bytes 393220
  7.2 24.6 %copy-start.12 = (s32[8,4]{0,1:T(4,128)S(1)}, s32[8,4]{0,1:T(4,128)}, u32[]{:S(2)}) copy-start(s32[8,4]{0,1:T(4,128)} %param.24) | copy-start | bytes 388
  7.2 25.3 %copy-start.1 = (s32[8]{0:T(128)S(1)}, s32[8]{0:T(128)}, u32[]{:S(2)}) copy-start(s32[8]{0:T(128)} %param.25) | copy-start | bytes 100
  7.2 27.3 %copy-start.11 = (bf16[256,256]{1,0:T(8,128)(2,1)S(1)}, bf16[256,256]{1,0:T(8,128)(2,1)}, u32[]{:S(2)}) copy-start(bf16[256,256]{1,0:T(8,128)(2,1)} %param.26) | copy-start | bytes 393220
  7.2 174.4 %all-reduce.5.cloned.1.call-start = ((), (), s32[]{:S(2)}) async-start(), calls=%async_computation | async-start | bytes 4718592 | tf_op jit(solution)/shard_map/psum | solution.py:174
  26.2 19.6 %collective-permute-start = (bf16[4,128,256]{2,1,0:T(8,128)(2,1)S(1)}, bf16[4,128,256]{2,1,0:T(8,128)(2,1)}, u32[]{:S(2)}, u32[]{:S(2)}) collective-permute-start(bf16[4,128,256]{2,1,0:T(8,128)(2,1)S(1)} %bitcast.196), channel_id=1, source_target_pairs={{12,0},{0,4},{4,8},{8,12},{13,1},{1,5},{5,9},{9,13},{14,2},{2,6},{... | collective-permute-start | bytes 786440 | tf_op jit(solution)/shard_map/ppermute | solution.py:17
  26.6 23.1 %collective-permute-start.2 = (bf16[4,128,256]{2,1,0:T(8,128)(2,1)S(1)}, bf16[4,128,256]{2,1,0:T(8,128)(2,1)}, u32[]{:S(2)}, u32[]{:S(2)}) collective-permute-start(bf16[4,128,256]{2,1,0:T(8,128)(2,1)S(1)} %bitcast.197), channel_id=1, source_target_pairs={{4,0},{8,4},{12,8},{0,12},{5,1},{9,5},{13,9},{1,13},{6,2},{10,6},{... | collective-permute-start | bytes 786440 | tf_op jit(solution)/shard_map/ppermute | solution.py:17
  28.3 31.7 %collective-permute-start.3 = (bf16[4,128,256]{2,1,0:T(8,128)(2,1)S(1)}, bf16[4,128,256]{2,1,0:T(8,128)(2,1)}, u32[]{:S(2)}, u32[]{:S(2)}) collective-permute-start(bf16[4,128,256]{2,1,0:T(8,128)(2,1)S(1)} %bitcast.194), channel_id=1, source_target_pairs={{4,0},{8,4},{12,8},{0,12},{5,1},{9,5},{13,9},{1,13},{6,2},{10,6},{... | collective-permute-start | bytes 786440 | tf_op jit(solution)/shard_map/ppermute | solution.py:17
  28.7 35.4 %collective-permute-start.1 = (bf16[4,128,256]{2,1,0:T(8,128)(2,1)S(1)}, bf16[4,128,256]{2,1,0:T(8,128)(2,1)}, u32[]{:S(2)}, u32[]{:S(2)}) collective-permute-start(bf16[4,128,256]{2,1,0:T(8,128)(2,1)S(1)} %bitcast.195), channel_id=1, source_target_pairs={{12,0},{0,4},{4,8},{8,12},{13,1},{1,5},{5,9},{9,13},{14,2},{2,6},{... | collective-permute-start | bytes 786440 | tf_op jit(solution)/shard_map/ppermute | solution.py:17
  50.8 2.9 %copy-start.2 = (f32[4,16,128,128]{3,2,1,0:T(8,128)S(1)}, f32[4,16,128,128]{3,2,1,0:T(8,128)}, u32[]{:S(2)}) copy-start(f32[4,16,128,128]{3,2,1,0:T(8,128)} %get-tuple-element.37) | copy-start | bytes 12582916
  50.8 5.0 %copy-start.3 = (f32[4,16,128,128]{3,2,1,0:T(8,128)S(1)}, f32[4,16,128,128]{3,2,1,0:T(8,128)}, u32[]{:S(2)}) copy-start(f32[4,16,128,128]{3,2,1,0:T(8,128)} %get-tuple-element.39) | copy-start | bytes 12582916
  51.8 6.3 %copy-start.4 = (f32[4,16,128,128]{3,2,1,0:T(8,128)}, f32[4,16,128,128]{3,2,1,0:T(8,128)S(1)}, u32[]{:S(2)}) copy-start(f32[4,16,128,128]{3,2,1,0:T(8,128)S(1)} %get-tuple-element.35) | copy-start | bytes 12582916
  55.8 2.3 copy-start.7
  65.3 3.6 %copy-start.13 = (bf16[256,256]{1,0:T(8,128)(2,1)S(1)}, bf16[256,256]{1,0:T(8,128)(2,1)}, u32[]{:S(2)}) copy-start(bf16[256,256]{1,0:T(8,128)(2,1)} %param.29) | copy-start | bytes 393220
  71.2 5.5 %copy-start.6 = (bf16[4,64,1024]{2,1,0:T(8,128)(2,1)S(1)}, bf16[4,64,1024]{2,1,0:T(8,128)(2,1)}, u32[]{:S(2)}) copy-start(bf16[4,64,1024]{2,1,0:T(8,128)(2,1)} %get-tuple-element.17) | copy-start | bytes 1572868
  78.8 0.8 copy-start.5
  84.0 155.2 %all-reduce.7.cloned.1.call-start = ((), (), s32[]{:S(2)}) async-start(), calls=%async_computation.1 | async-start | bytes 4718592 | tf_op jit(solution)/shard_map/psum | solution.py:174
  239.1 3.3 %copy-start.8 = (f32[256,256]{1,0:T(8,128)S(1)}, f32[256,256]{1,0:T(8,128)}, u32[]{:S(2)}) copy-start(f32[256,256]{1,0:T(8,128)} %get-tuple-element.10) | copy-start | bytes 786436
Sparse Core Ops, SparseCore 0:
  84.1 97.4 all-reduce.4
  184.1 54.9 all-reduce.6
